TPU v7x, 32 devices: a whole 2x2x4 slice. The times are simulated.
32 devices in a mesh: dp: 16 (over z, y, core), mp: 2 (over x).
Axes of the slice: x: 2, y: 2, z: 4, core: 2. Of those that a mesh axis runs over, the one named last changes fastest.
Arguments:
- patch_counts: int32 [128], P('dp'), may hold values from 100 to 240, as said below
- tokens: bfloat16 [128, 280, 768], P('dp'), may hold values from -6 to 6
- cotangent: bfloat16 [128, 280, 768], P('dp'), may hold values from -6 to 6
- attn_gain: float32 [768], P('dp'), may hold values from 0.1 to 1.9
- attn_shift: float32 [768], P('dp'), may hold values from -1.75 to 1.75
- w_qkv: float32 [768, 3, 768], P('dp', None, 'mp'), may hold values from -0.21875 to 0.21875
- b_qv: float32 [2, 768], P(None, 'mp'), may hold values from -3 to 3
- w_proj: float32 [768, 768], P('mp', 'dp'), may hold values from -0.875 to 0.875
- b_proj: float32 [768], P('dp'), may hold values from -3 to 3
- ffn_gain: float32 [768], P('dp'), may hold values from 0.1 to 1.9
- ffn_shift: float32 [768], P('dp'), may hold values from -1.75 to 1.75
- w_up: float32 [768, 3072], P('dp', 'mp'), may hold values from -0.21875 to 0.21875
- b_up: float32 [3072], P('mp'), may hold values from -3 to 3
- w_down: float32 [3072, 768], P('mp', 'dp'), may hold values from -0.109375 to 0.109375
- b_down: float32 [768], P('dp'), may hold values from -3 to 3
Outputs:
- block_out: bfloat16 [128, 280, 768], P('dp')
- tokens_grad: bfloat16 [128, 280, 768], P('dp')
- attn_gain_grad: float32 [768], P('dp')
- attn_shift_grad: float32 [768], P('dp')
- w_qkv_grad: float32 [768, 3, 768], P('dp', None, 'mp')
- b_qv_grad: float32 [2, 768], P(None, 'mp')
- w_proj_grad: float32 [768, 768], P('mp', 'dp')
- b_proj_grad: float32 [768], P('dp')
- ffn_gain_grad: float32 [768], P('dp')
- ffn_shift_grad: float32 [768], P('dp')
- w_up_grad: float32 [768, 3072], P('dp', 'mp')
- b_up_grad: float32 [3072], P('mp')
- w_down_grad: float32 [3072, 768], P('mp', 'dp')
- b_down_grad: float32 [768], P('dp')
Inputs may be any that keep to these rules, and one draw needn't show every extreme that they name: `patch_counts`: patch count of each pair; in every draw some pair has exactly 240 patches and some exactly 100.
All inputs are finite; a program needn't handle non-finite values.
Results may differ from a plain program's by a relative error of at most 0.022.
Values may be sent and summed in bfloat16 or wider, within the bound.
A program may use at most 192 MiB of HBM per device.

v0:
```python
import math
import jax
import jax.numpy as jnp
from jax import lax
from jax.sharding import PartitionSpec as P

HEADS = 12
HEAD_DIM = 64
TEXT = 40


def normalize(values, gain, shift):
    center = values - jnp.mean(values, axis=-1, keepdims=True)
    spread = jnp.mean(center * center, axis=-1, keepdims=True)
    return center * lax.rsqrt(spread + 1e-06) * gain + shift


def norm_back(values, gain, incoming):
    _, pullback = jax.vjp(lambda member, scaling: normalize(member, scaling, 0.0), values, gain)
    d_values, d_gain = pullback(incoming)
    return (d_values, d_gain, jnp.sum(incoming, axis=(0, 1)))


def per_device(
    patch_counts,
    tokens,
    cotangent,
    attn_gain,
    attn_shift,
    w_qkv,
    b_qv,
    w_proj,
    b_proj,
    ffn_gain,
    ffn_shift,
    w_up,
    b_up,
    w_down,
    b_down,
):
    low_type = jnp.bfloat16
    pair_count, rows_pair, _ = tokens.shape
    head_count = HEADS // lax.axis_size("mp")
    local_width = w_qkv.shape[2]
    score_scale = HEAD_DIM ** (-0.5)
    pair_block = math.gcd(pair_count, -(-512 // rows_pair))
    block_count = pair_count // pair_block
    gathered = (
        lax.all_gather(w_qkv.astype(low_type), "dp", axis=0, tiled=True),
        lax.all_gather(w_proj.astype(low_type), "dp", axis=1, tiled=True),
        lax.all_gather(w_up.astype(low_type), "dp", axis=0, tiled=True),
        lax.all_gather(w_down.astype(low_type), "dp", axis=1, tiled=True),
        lax.all_gather(attn_gain.astype(low_type), "dp", axis=0, tiled=True),
        lax.all_gather(attn_shift.astype(low_type), "dp", axis=0, tiled=True),
        lax.all_gather(b_proj.astype(low_type), "dp", axis=0, tiled=True),
        lax.all_gather(ffn_gain.astype(low_type), "dp", axis=0, tiled=True),
        lax.all_gather(ffn_shift.astype(low_type), "dp", axis=0, tiled=True),
        lax.all_gather(b_down.astype(low_type), "dp", axis=0, tiled=True),
    )
    qkv_full, proj_full, up_full, down_full = (gathered[0], gathered[1], gathered[2], gathered[3])
    gain_one = gathered[4].astype(jnp.float32)
    shift_one = gathered[5].astype(jnp.float32)
    proj_bias = gathered[6].astype(jnp.float32)
    gain_two = gathered[7].astype(jnp.float32)
    shift_two = gathered[8].astype(jnp.float32)
    down_bias = gathered[9].astype(jnp.float32)
    bias_qv = b_qv.astype(low_type).astype(jnp.float32)
    up_bias = b_up.astype(low_type).astype(jnp.float32)
    row_valid = (
        jnp.arange(rows_pair, dtype=jnp.int32)[None, :] < (TEXT + patch_counts)[:, None]
    ).astype(jnp.float32)
    inputs = tokens.astype(jnp.float32)
    normed_one = normalize(inputs, gain_one, shift_one).astype(low_type)
    qkv = jnp.einsum("psd,dtc->pstc", normed_one, qkv_full, preferred_element_type=jnp.float32)
    queries = (qkv[:, :, 0] + bias_qv[0]).astype(low_type)
    key_rows = qkv[:, :, 1].astype(low_type)
    values = (qkv[:, :, 2] + bias_qv[1]).astype(low_type)

    def by_blocks(array):
        return array.reshape(block_count, pair_block, rows_pair, head_count, HEAD_DIM)

    key_mask = row_valid.reshape(block_count, pair_block, rows_pair)

    def score_rows(query_block, key_block, mask_block):
        raw = (
            jnp.einsum(
                "bqhe,bkhe->bhqk", query_block, key_block, preferred_element_type=jnp.float32
            )
            * score_scale
        )
        return jnp.where(mask_block[:, None, None, :] > 0, raw, -1e30)

    def attend(operands):
        query_block, key_block, value_block, mask_block = operands
        scores = score_rows(query_block, key_block, mask_block)
        row_max = jnp.max(scores, axis=-1, keepdims=True)
        expo = jnp.exp(scores - row_max)
        row_total = jnp.sum(expo, axis=-1, keepdims=True)
        probabilities = (expo / row_total).astype(low_type)
        attended_block = jnp.einsum(
            "bhqk,bkhe->bqhe", probabilities, value_block, preferred_element_type=jnp.float32
        ).astype(low_type)
        log_total = row_max[..., 0] + jnp.log(row_total[..., 0])
        return (attended_block, log_total)

    attended_blocks, log_totals = lax.map(
        attend, (by_blocks(queries), by_blocks(key_rows), by_blocks(values), key_mask)
    )
    attended = attended_blocks.reshape(pair_count, rows_pair, local_width)
    proj_part = jnp.einsum("psc,cd->psd", attended, proj_full, preferred_element_type=jnp.float32)
    attn_sum = lax.psum(proj_part.astype(jnp.bfloat16), "mp").astype(jnp.float32)
    hidden = inputs + attn_sum + proj_bias
    normed_two = normalize(hidden, gain_two, shift_two).astype(low_type)
    pre_act = (
        jnp.einsum("psd,df->psf", normed_two, up_full, preferred_element_type=jnp.float32) + up_bias
    )
    active = jax.nn.gelu(pre_act, approximate=False).astype(low_type)
    down_part = jnp.einsum("psf,fd->psd", active, down_full, preferred_element_type=jnp.float32)
    mlp_sum = lax.psum(down_part.astype(jnp.bfloat16), "mp").astype(jnp.float32)
    block_out = ((hidden + mlp_sum + down_bias) * row_valid[:, :, None]).astype(low_type)
    qkv_back, proj_back, up_back, down_back = (qkv_full, proj_full, up_full, down_full)
    gain_one_back, gain_two_back = (gain_one, gain_two)
    upstream = cotangent.astype(jnp.float32) * row_valid[:, :, None]
    upstream_low = upstream.astype(low_type)
    grad_b_down = jnp.sum(upstream, axis=(0, 1))
    grad_w_down = jnp.einsum(
        "psf,psd->fd", active, upstream_low, preferred_element_type=jnp.float32
    )
    d_active = jnp.einsum(
        "psd,fd->psf", upstream_low, down_back, preferred_element_type=jnp.float32
    )
    _, gelu_pull = jax.vjp(lambda member: jax.nn.gelu(member, approximate=False), pre_act)
    d_pre = gelu_pull(d_active)[0].astype(low_type)
    grad_b_up = jnp.sum(d_pre, axis=(0, 1), dtype=jnp.float32)
    grad_w_up = jnp.einsum("psd,psf->df", normed_two, d_pre, preferred_element_type=jnp.float32)
    d_normed_two = lax.psum(
        jnp.einsum("psf,df->psd", d_pre, up_back, preferred_element_type=jnp.float32).astype(
            jnp.bfloat16
        ),
        "mp",
    ).astype(jnp.float32)
    d_hidden_norm, grad_gain_two, grad_shift_two = norm_back(hidden, gain_two_back, d_normed_two)
    d_hidden = upstream + d_hidden_norm
    grad_b_proj = jnp.sum(d_hidden, axis=(0, 1))
    d_hidden_low = d_hidden.astype(low_type)
    grad_w_proj = jnp.einsum(
        "psc,psd->cd", attended, d_hidden_low, preferred_element_type=jnp.float32
    )
    d_attended = jnp.einsum(
        "psd,cd->psc", d_hidden_low, proj_back, preferred_element_type=jnp.float32
    ).astype(low_type)

    def attend_back(operands):
        query_block, key_block, value_block, mask_block, log_total, d_out = operands
        scores = score_rows(query_block, key_block, mask_block)
        probabilities = jnp.exp(scores - log_total[..., None])
        d_probs = jnp.einsum(
            "bqhe,bkhe->bhqk", d_out, value_block, preferred_element_type=jnp.float32
        )
        d_value = jnp.einsum(
            "bhqk,bqhe->bkhe",
            probabilities.astype(low_type),
            d_out,
            preferred_element_type=jnp.float32,
        )
        inner = jnp.sum(probabilities * d_probs, axis=-1, keepdims=True)
        d_scores = (probabilities * (d_probs - inner)).astype(low_type)
        d_query = score_scale * jnp.einsum(
            "bhqk,bkhe->bqhe", d_scores, key_block, preferred_element_type=jnp.float32
        )
        d_key = score_scale * jnp.einsum(
            "bhqk,bqhe->bkhe", d_scores, query_block, preferred_element_type=jnp.float32
        )
        return jnp.stack([d_query, d_key, d_value], axis=2).astype(low_type)

    d_blocks = lax.map(
        attend_back,
        (
            by_blocks(queries),
            by_blocks(key_rows),
            by_blocks(values),
            key_mask,
            log_totals,
            by_blocks(d_attended),
        ),
    )
    d_qkv = d_blocks.reshape(pair_count, rows_pair, 3, local_width)
    column_sums = jnp.sum(d_qkv, axis=(0, 1), dtype=jnp.float32)
    grad_b_qv = jnp.stack([column_sums[0], column_sums[2]], axis=0)
    grad_w_qkv = jnp.einsum("psd,pstc->dtc", normed_one, d_qkv, preferred_element_type=jnp.float32)
    d_normed_one = lax.psum(
        jnp.einsum("pstc,dtc->psd", d_qkv, qkv_back, preferred_element_type=jnp.float32).astype(
            jnp.bfloat16
        ),
        "mp",
    ).astype(jnp.float32)
    d_input_norm, grad_gain_one, grad_shift_one = norm_back(inputs, gain_one_back, d_normed_one)
    tokens_grad = (d_hidden + d_input_norm).astype(low_type)
    bias_grads = lax.psum((grad_b_qv, grad_b_up), "dp")
    summed = (
        lax.psum_scatter(grad_w_qkv, "dp", scatter_dimension=0, tiled=True),
        lax.psum_scatter(grad_w_proj, "dp", scatter_dimension=1, tiled=True),
        lax.psum_scatter(grad_w_up, "dp", scatter_dimension=0, tiled=True),
        lax.psum_scatter(grad_w_down, "dp", scatter_dimension=1, tiled=True),
        lax.psum_scatter(grad_gain_one, "dp", scatter_dimension=0, tiled=True),
        lax.psum_scatter(grad_shift_one, "dp", scatter_dimension=0, tiled=True),
        lax.psum_scatter(grad_b_proj, "dp", scatter_dimension=0, tiled=True),
        lax.psum_scatter(grad_gain_two, "dp", scatter_dimension=0, tiled=True),
        lax.psum_scatter(grad_shift_two, "dp", scatter_dimension=0, tiled=True),
        lax.psum_scatter(grad_b_down, "dp", scatter_dimension=0, tiled=True),
    )
    out_qkv, out_proj, out_up, out_down = (summed[0], summed[1], summed[2], summed[3])
    out_gain_one, out_shift_one, out_bproj = (summed[4], summed[5], summed[6])
    out_gain_two, out_shift_two, out_bdown = (summed[7], summed[8], summed[9])
    return (
        block_out,
        tokens_grad,
        out_gain_one,
        out_shift_one,
        out_qkv,
        bias_grads[0],
        out_proj,
        out_bproj,
        out_gain_two,
        out_shift_two,
        out_up,
        bias_grads[1],
        out_down,
        out_bdown,
    )


def solution(mesh):
    in_specs = (
        P("dp"),
        P("dp", None, None),
        P("dp", None, None),
        P("dp"),
        P("dp"),
        P("dp", None, "mp"),
        P(None, "mp"),
        P("mp", "dp"),
        P("dp"),
        P("dp"),
        P("dp"),
        P("dp", "mp"),
        P("mp"),
        P("mp", "dp"),
        P("dp"),
    )
    out_specs = (
        P("dp", None, None),
        P("dp", None, None),
        P("dp"),
        P("dp"),
        P("dp", None, "mp"),
        P(None, "mp"),
        P("mp", "dp"),
        P("dp"),
        P("dp"),
        P("dp"),
        P("dp", "mp"),
        P("mp"),
        P("mp", "dp"),
        P("dp"),
    )
    return jax.shard_map(
        per_device, mesh=mesh, in_specs=in_specs, out_specs=out_specs, check_vma=False
    )
```

profile of v0, /device:TPU:0, one launch (start us, length us, event | category | flops | bytes accessed | tf_op | source)
XLA Modules:
  0.0 1070.2 jit_solution(13060933296893398383)
XLA Ops:
  20.8 63.2 %all-reduce.13 = (bf16[768]{0:T(1024)(128)(2,1)}, bf16[768]{0:T(1024)(128)(2,1)}, bf16[768]{0:T(1024)(128)(2,1)}, bf16[768]{0:T(1024)(128)(2,1)}, bf16[768]{0:T(1024)(128)(2,1)}, /*index=5*/bf16[768]{0:T(1024)(128)(2,1)}) all-reduce(bf16[768]{0:T(1024)(128)(2,1)} %dynamic-update-slice.4, ...), channel_id=1, replica_groups=mesh['dp'=16,'mp'=2] {'dp'}, use_global_device_ids=true, to_apply=%add.4 | all-reduce | flops 4608 | bytes 18432
  97.2 20.3 %all_gather.33 = bf16[384,768]{0,1:T(8,128)(2,1)} all-gather(bf16[384,48]{0,1:T(8,128)(2,1)S(1)} %convert_element_type.183), channel_id=1, replica_groups=mesh['dp'=16,'mp'=2] {'dp'}, dimensions={1}, use_global_device_ids=true | all-gather | bytes 626688 | tf_op jit(solution)/shard_map/all_gather | solution.py:50
  117.5 7.1 fusion.96
  129.4 6.0 copy.58
  135.3 5.5 copy.59
  144.8 7.3 add_convert_fusion.3
  152.2 32.6 %while.22 = (s32[]{:T(128)}, bf16[4,2,280,6,64]{2,4,3,1,0:T(8,128)(2,1)}, f32[4,2,6,280]{3,2,1,0:T(8,128)S(1)}, bf16[4,2,280,6,64]{2,4,3,1,0:T(8,128)(2,1)}, f32...) while((s32[]{:T(128)}, ...), condition=%wide.region_5.6_spmd, body=%wide.region_2.5_spmd.sunk | while | flops 252346640 | bytes 13796445 | solution.py:106
  184.8 6.0 convolution_convert_fusion.2
  198.1 83.8 %all-reduce.19.cloned.1.call-done = bf16[8,280,768]{2,1,0:T(8,128)(2,1)} async-done(((bf16[8,280,768]{2,1,0:T(8,128)(2,1)}), bf16[8,280,768]{2,1,0:T(8,128)(2,1)}) %all-reduce.19.cloned.1.call-update) | async-done | bytes 3440656 | tf_op jit(solution)/shard_map/psum | solution.py:111
  288.5 38.6 %all-gather.6.cloned.1.call-done = bf16[768,1536]{1,0:T(8,128)(2,1)} async-done(((bf16[48,1536]{1,0:T(8,128)(2,1)}), bf16[768,1536]{1,0:T(8,128)(2,1)}) %all-gather.6.cloned.1.call-update) | async-done | bytes 2359312 | tf_op jit(solution)/shard_map/all_gather | solution.py:51
  327.1 13.9 %fusion.86 = (u8[280,1536]{1,0:T(8,128)(4,1)S(1)}, u8[280,1536]{1,0:T(8,128)(4,1)S(1)}, f32[8,280,1536]{2,1,0:T(8,128)S(1)}) fusion(f32[1536]{0:T(1024)} %convert_convert_fusion, bf16[768,1536]{1,0:T(8,128)(2,1)} %all-gather.6.cloned.1.call-done, f32[768]{0:T(1024)} %convert_element_type.191, f32[768]{0:T(1024)} %convert_element_type.189, ...), kind=kOutput, calls=%fused_computation.134 | convolution fusion | flops 5347614720 | bytes 23896576 | tf_op jit(solution)/shard_map/psd,df->psf/dot_general | solution.py:115
  341.0 4.9 copy-done.6
  346.0 32.9 %multiply_convert_fusion.1 = (bf16[8,280,1536]{2,1,0:T(8,128)(2,1)}, f32[8,280,1536]{2,1,0:T(8,128)}) fusion(f32[8,280,1536]{2,1,0:T(8,128)S(1)} %get-tuple-element.187, f32[1536]{0:T(1024)S(1)} %copy-done.25, u8[280,1536]{1,0:T(8,128)(4,1)S(1)} %get-tuple-element.113, u8[280,1536]{1,0:T(8,128)(4,1)S(1)} %get-tuple-element.112), kind=kLoop, calls=%fused_computation.75 | loop fusion | flops 244285440 | bytes 35272704 | tf_op jit(solution)/shard_map/convert_element_type | solution.py:117
  378.9 18.8 %convert_reduce_fusion.1 = (f32[1536]{0:T(1024)}, bf16[8,280,1536]{2,1,0:T(8,128)(2,1)}) fusion(f32[8,280,1536]{2,1,0:T(8,128)} %get-tuple-element.173, bf16[1536,768]{0,1:T(8,128)(2,1)} %all-gather.8.cloned.1.call-done, bf16[8,280,768]{2,1,0:T(8,128)(2,1)} %param.21, f32[8,280]{1,0:T(8,128)} %fusion.108, f32[8,280,1536]{2,1,0:T(8,128)} %copy-done.6, ...), kind=kOutput, calls=%fused_computation.73 | convolution fusion | flops 5348473344 | bytes 40227584 | tf_op jit(solution)/shard_map/psd,fd->psf/dot_general | solution.py:129
  397.6 10.0 convolution_convert_fusion
  407.7 10.0 convolution_convert_fusion.1
  417.7 81.1 %all-reduce.21.cloned.1.call-done = bf16[8,280,768]{2,1,0:T(8,128)(2,1)} async-done(((bf16[8,280,768]{2,1,0:T(8,128)(2,1)}), bf16[8,280,768]{2,1,0:T(8,128)(2,1)}) %all-reduce.21.cloned.1.call-update) | async-done | bytes 3440656 | tf_op jit(solution)/shard_map/psum | solution.py:136
  498.8 6.4 convert_reduce_fusion.3
  505.2 5.6 fusion.77
  510.8 4.9 fusion.111
  525.6 64.1 %while.23 = (s32[]{:T(128)}, bf16[4,2,280,3,6,64]{2,5,4,1,3,0:T(8,128)(2,1)}, bf16[4,2,280,6,64]{2,4,3,1,0:T(8,128)(2,1)}, f32[4,2,280]{2,1,0:T(2,128)}, bf16[4,...) while((s32[]{:T(128)}, ...), condition=%wide.region_15.16_spmd, body=%wide.region_13.15_spmd.sunk | while | flops 621167104 | bytes 36805476 | solution.py:176
  596.9 7.7 bitcast_convert_fusion
  604.8 7.4 fusion.101
  612.3 12.6 %convolution_bitcast_fusion.1 = f32[768,1536]{1,0:T(8,128)} fusion(bf16[8,280,1536]{2,1,0:T(8,128)(2,1)} %get-tuple-element.189, f32[768]{0:T(1024)S(1)} %copy-done.35, f32[768]{0:T(1024)S(1)} %copy-done.24, f32[8,280]{1,0:T(8,128)S(1)} %copy-done.20, f32[8,280]{1,0:T(8,128)S(1)} %broadcast_multiply_fusion, f32[768]{0:T(1024)S(1)} %convert_element_type.187, ...), kind=kOutput, calls=%fused_computation.130 | convolution fusion | flops 5300305920 | bytes 18508288 | tf_op jit(solution)/shard_map/psd,psf->df/dot_general | solution.py:135
  625.0 11.0 %convolution_bitcast_fusion = f32[1536,768]{0,1:T(8,128)} fusion(bf16[8,280,1536]{2,1,0:T(8,128)(2,1)} %get-tuple-element.172, bf16[8,280,768]{2,1,0:T(8,128)(2,1)} %param.21, f32[8,280]{1,0:T(8,128)S(1)} %copy-done.18), kind=kOutput, calls=%fused_computation.129 | convolution fusion | flops 5289984000 | bytes 15049472 | tf_op jit(solution)/shard_map/psf,psd->fd/dot_general | solution.py:126
  636.3 13.7 %convolution_bitcast_fusion.2 = f32[768,3,384]{2,0,1:T(8,128)} fusion(bf16[8,280,3,384]{1,3,2,0:T(8,128)(2,1)} %bitcast.170, bf16[8,280,768]{2,1,0:T(8,128)(2,1)S(1)} %copy-done, f32[768]{0:T(1024)S(1)} %copy-done.34, f32[768]{0:T(1024)S(1)} %copy-done.22, f32[8,280]{1,0:T(8,128)S(1)} %copy-done.16, f32[8,280]{1,0:T(8,128)S(1)} %copy-done.11), kind=kOutput, calls=%fused_computation.144 | convolution fusion | flops 3973939200 | bytes 12164608 | tf_op jit(solution)/shard_map/psd,pstc->dtc/dot_general | solution.py:190
  655.3 115.5 %all-reduce.23.cloned.1.call-done = (bf16[8,280,768]{2,1,0:T(8,128)(2,1)}, bf16[8,280,768]{2,1,0:T(8,128)(2,1)}) async-done(((bf16[8,280,768]{2,1,0:T(8,128)(2,1)}, bf16[8,280,768]{2,1,0:T(8,128)(2,1)}), (bf16[8,280,768]{2,1,0:T(8,128)(2,1)}, bf16[8,280,768]{2,1,0:T(8,128)(2,1)})) %all-reduce.23.cloned.1.call-update) | async-done | bytes 6881296 | tf_op jit(solution)/shard_map/psum | solution.py:119
  779.3 61.8 %all-reduce.12 = (f32[768]{0:T(1024)S(1)}, f32[768]{0:T(1024)S(1)}, f32[2,384]{1,0:T(2,128)}, f32[768]{0:T(1024)}, f32[768]{0:T(1024)}, /*index=5*/f32[768]{0:T(1024)}, f32[1536]{0:T(1024)}, f32[768]{0:T(1024)S(1)}) all-reduce(f32[768]{0:T(1024)S(1)} %get-tuple-element.116, ...), channel_id=2, replica_groups=mesh['dp'=16,'mp'=2] {'dp'}, use_global_device_ids=true, to_apply=%region_20.21.clone | all-reduce | flops 6912 | bytes 55296
  846.6 11.0 %add_convert_fusion.1 = (bf16[8,280,768]{2,1,0:T(8,128)(2,1)}, bf16[8,280,768]{2,1,0:T(8,128)(2,1)}) fusion(f32[8,280,768]{2,1,0:T(8,128)} %copy-done.3, bf16[8,280,768]{2,1,0:T(8,128)(2,1)S(1)} %copy-done, bf16[8,280,768]{2,1,0:T(8,128)(2,1)} %get-tuple-element.169, f32[8,280]{1,0:T(8,128)S(1)} %negate_multiply_fusion.1, ...), kind=kLoop, calls=%fused_computation.116 | loop fusion | flops 32686080 | bytes 27579136 | tf_op jit(solution)/shard_map/convert_element_type | solution.py:198
  857.6 54.7 %reduce-scatter.9.cloned.1.call-done = f32[48,1536]{1,0:T(8,128)} async-done(((f32[768,1536]{1,0:T(8,128)}), f32[48,1536]{1,0:T(8,128)}) %reduce-scatter.9.cloned.1.call-update) | async-done | bytes 294928 | tf_op jit(solution)/shard_map/reduce_scatter | solution.py:203
  912.3 79.2 %reduce-scatter.11.cloned.1.call-done = f32[1536,48]{0,1:T(8,128)} async-done(((f32[1536,768]{0,1:T(8,128)}), f32[1536,48]{0,1:T(8,128)}) %reduce-scatter.11.cloned.1.call-update) | async-done | bytes 294928 | tf_op jit(solution)/shard_map/reduce_scatter | solution.py:204
  991.5 71.6 %reduce-scatter.5.cloned.1.call-done = f32[48,3,384]{2,0,1:T(8,128)} async-done(((f32[768,3,384]{2,0,1:T(8,128)}), f32[48,3,384]{2,0,1:T(8,128)}) %reduce-scatter.5.cloned.1.call-update) | async-done | bytes 221200 | tf_op jit(solution)/shard_map/reduce_scatter | solution.py:201
  (234 shorter events, 181.1 us)
Async XLA Ops:
  7.2 110.4 %copy-start = (bf16[8,280,768]{2,1,0:T(8,128)(2,1)S(1)}, bf16[8,280,768]{2,1,0:T(8,128)(2,1)}, u32[]{:S(2)}) copy-start(bf16[8,280,768]{2,1,0:T(8,128)(2,1)} %param.20) | copy-start | bytes 10321924
  7.2 110.3 %all-gather.4.cloned.1.call-start = ((), (), s32[]{:S(2)}) async-start(), calls=%async_computation.4 | async-start | bytes 1880064 | tf_op jit(solution)/shard_map/all_gather | solution.py:49
  9.0 272.9 %all-reduce.19.cloned.1.call-start = ((), (), s32[]{:S(2)}) async-start(), calls=%async_computation.5 | async-start | bytes 6881280 | tf_op jit(solution)/shard_map/psum | solution.py:111
  84.7 39.9 %copy-start.21 = (f32[768]{0:T(1024)}, f32[768]{0:T(1024)S(1)}, u32[]{:S(2)}) copy-start(f32[768]{0:T(1024)S(1)} %convert_element_type.172) | copy-start | bytes 9220
  92.9 31.7 %copy-start.10 = (f32[8,280]{1,0:T(8,128)}, f32[8,280]{1,0:T(8,128)S(1)}, u32[]{:S(2)}) copy-start(f32[8,280]{1,0:T(8,128)S(1)} %broadcast_multiply_fusion.1) | copy-start | bytes 26884
  135.3 9.5 copy-start.28
  135.3 9.5 copy-start.29
  184.8 9.5 copy-start.39
  184.8 12.1 %copy-start.37 = (bf16[768]{0:T(1024)(128)(2,1)S(1)}, bf16[768]{0:T(1024)(128)(2,1)}, u32[]{:S(2)}) copy-start(bf16[768]{0:T(1024)(128)(2,1)} %get-tuple-element.162) | copy-start | bytes 4612
  184.8 12.7 %copy-start.32 = (f32[1536]{0:T(1024)S(1)}, f32[1536]{0:T(1024)}, u32[]{:S(2)}) copy-start(f32[1536]{0:T(1024)} %param.31) | copy-start | bytes 18436
  190.8 136.3 %all-gather.6.cloned.1.call-start = ((), (), s32[]{:S(2)}) async-start(), calls=%async_computation.6 | async-start | bytes 2506752 | tf_op jit(solution)/shard_map/all_gather | solution.py:51
  192.5 186.3 %all-gather.8.cloned.1.call-start = ((), (), s32[]{:S(2)}) async-start(), calls=%async_computation.7 | async-start | bytes 2506752 | tf_op jit(solution)/shard_map/all_gather | solution.py:52
  194.2 304.6 %all-reduce.21.cloned.1.call-start = ((), (), s32[]{:S(2)}) async-start(), calls=%async_computation.8 | async-start | bytes 6881280 | tf_op jit(solution)/shard_map/psum | solution.py:136
  327.1 18.9 %copy-start.25 = (f32[1536]{0:T(1024)S(1)}, f32[1536]{0:T(1024)}, u32[]{:S(2)}) copy-start(f32[1536]{0:T(1024)} %convert_convert_fusion) | copy-start | bytes 18436
  378.9 18.8 %copy-start.40 = (bf16[768,1536]{1,0:T(8,128)(2,1)S(1)}, bf16[768,1536]{1,0:T(8,128)(2,1)}, u32[]{:S(2)}) copy-start(bf16[768,1536]{1,0:T(8,128)(2,1)} %all-gather.6.cloned.1.call-done) | copy-start | bytes 7077892
  407.7 363.0 %all-reduce.23.cloned.1.call-start = ((), (), s32[]{:S(2)}) async-start(), calls=%async_computation.13 | async-start | bytes 13762560 | tf_op jit(solution)/shard_map/psum | solution.py:119
  604.6 7.7 copy-start.20
  604.6 253.0 %reduce-scatter.7.cloned.1.call-start = ((), (), s32[]{:S(2)}) async-start(), calls=%async_computation.10 | async-start | bytes 1253376 | tf_op jit(solution)/shard_map/reduce_scatter | solution.py:202
  612.2 12.8 %copy-start.18 = (f32[8,280]{1,0:T(8,128)S(1)}, f32[8,280]{1,0:T(8,128)}, u32[]{:S(2)}) copy-start(f32[8,280]{1,0:T(8,128)} %fusion.108) | copy-start | bytes 26884
  612.2 300.1 %reduce-scatter.9.cloned.1.call-start = ((), (), s32[]{:S(2)}) async-start(), calls=%async_computation.11 | async-start | bytes 5013504 | tf_op jit(solution)/shard_map/reduce_scatter | solution.py:203
  624.9 11.4 %copy-start.11 = (f32[8,280]{1,0:T(8,128)S(1)}, f32[8,280]{1,0:T(8,128)}, u32[]{:S(2)}) copy-start(f32[8,280]{1,0:T(8,128)} %copy-done.10) | copy-start | bytes 26884
  624.9 11.4 %copy-start.16 = (f32[8,280]{1,0:T(8,128)S(1)}, f32[8,280]{1,0:T(8,128)}, u32[]{:S(2)}) copy-start(f32[8,280]{1,0:T(8,128)} %fusion.109) | copy-start | bytes 26884
  624.9 11.4 %copy-start.22 = (f32[768]{0:T(1024)S(1)}, f32[768]{0:T(1024)}, u32[]{:S(2)}) copy-start(f32[768]{0:T(1024)} %copy-done.21) | copy-start | bytes 9220
  624.9 11.4 %copy-start.34 = (f32[768]{0:T(1024)S(1)}, f32[768]{0:T(1024)}, u32[]{:S(2)}) copy-start(f32[768]{0:T(1024)} %convert_element_type.174) | copy-start | bytes 9220
  624.9 366.6 %reduce-scatter.11.cloned.1.call-start = ((), (), s32[]{:S(2)}) async-start(), calls=%async_computation.12 | async-start | bytes 5013504 | tf_op jit(solution)/shard_map/reduce_scatter | solution.py:204
  636.0 14.1 %copy-start.36 = (bf16[768]{0:T(1024)(128)(2,1)S(1)}, bf16[768]{0:T(1024)(128)(2,1)}, u32[]{:S(2)}) copy-start(bf16[768]{0:T(1024)(128)(2,1)} %get-tuple-element.167) | copy-start | bytes 4612
  636.0 427.1 %reduce-scatter.5.cloned.1.call-start = ((), (), s32[]{:S(2)}) async-start(), calls=%async_computation.9 | async-start | bytes 3760128 | tf_op jit(solution)/shard_map/reduce_scatter | solution.py:201
  650.7 124.2 %copy-start.13 = (f32[8,280]{1,0:T(8,128)S(1)}, f32[8,280]{1,0:T(8,128)}, u32[]{:S(2)}) copy-start(f32[8,280]{1,0:T(8,128)} %copy-done.12) | copy-start | bytes 26884
  770.7 8.5 copy-start.26
  770.7 8.5 copy-start.27
  770.7 8.5 copy-start.30
  770.7 8.5 copy-start.31
  (20 other events, 95.2 us)
Sparse Core Ops, SparseCore 0:
  10.9 43.1 all-gather.3
  190.9 90.9 all-reduce.18
  284.8 42.3 all-gather.5
  329.8 41.0 all-gather.7
  407.8 90.9 all-reduce.20
  604.7 165.9 all-reduce.22
  774.9 58.1 reduce-scatter.6
  837.6 74.6 reduce-scatter.8
  916.7 74.7 reduce-scatter.10
  995.8 67.3 reduce-scatter.4
where the time goes:
time: 1080 us; the launch traced here: 1070 us
  waiting for transfers between devices  525 us (49%)
  matrix products  194 us (18%)
  blocking collectives  145 us (13%)
  other arithmetic  136 us (13%)
  local copies, waits for them, and re-layouts  53.1 us (5%)
  between operations  16.2 us (2%)
    unnamed x2, blocking collectives  125 us
    psum x1, waiting for transfers between devices, per_device(): mlp_sum = lax.psum(down_part.astype(jnp.bfloat16), 'mp').astype(jnp.float32)  115 us
    psum x1, waiting for transfers between devices, per_device(): lax.psum(proj_part.astype(jnp.bfloat16), 'mp').astype(jnp.float32)  83.8 us
    psum x1, waiting for transfers between devices, per_device(): lax.psum(jnp.einsum('psf,df->psd', d_pre, up_back, preferred_element_type...  81.1 us
    reduce_scatter x1, waiting for transfers between devices, per_device(): lax.psum_scatter(grad_w_down, 'dp', scatter_dimension=1, tiled=True)  79.2 us
    reduce_scatter x1, waiting for transfers between devices, per_device(): lax.psum_scatter(grad_w_qkv, 'dp', scatter_dimension=0, tiled=True)  71.6 us
    reduce_scatter x1, waiting for transfers between devices, per_device(): lax.psum_scatter(grad_w_up, 'dp', scatter_dimension=0, tiled=True)  54.7 us
    all_gather x1, waiting for transfers between devices, per_device(): lax.all_gather(w_up.astype(low_type), 'dp', axis=0, tiled=True)  38.6 us
  transfers between devices with their start and end apart: 10, of which 7 were waited for; matrix products, arithmetic and copies ran while one was open for 16% of the time, Pallas kernels for 0%

commit v1 on v0

--- a/solution.py
+++ b/solution.py
@@ -7,6 +7,22 @@
 HEADS = 12
 HEAD_DIM = 64
 TEXT = 40
+
+
+def ring_gather(x, axis, dim):
+    ways, here, hop = (lax.axis_size(axis), lax.axis_index(axis), x.shape[dim])
+    shape = [n * ways if d == dim else n for d, n in enumerate(x.shape)]
+    full = lax.dynamic_update_slice_in_dim(jnp.zeros(shape, x.dtype), x, here * hop, axis=dim)
+    going_up = going_down = x
+    for far in range(1, ways // 2 + 1):
+        going_up = lax.ppermute(going_up, axis, [(d, (d + 1) % ways) for d in range(ways)])
+        full = lax.dynamic_update_slice_in_dim(full, going_up, (here - far) % ways * hop, axis=dim)
+        if 2 * far < ways:
+            going_down = lax.ppermute(going_down, axis, [(d, (d - 1) % ways) for d in range(ways)])
+            full = lax.dynamic_update_slice_in_dim(
+                full, going_down, (here + far) % ways * hop, axis=dim
+            )
+    return full
 
 
 def normalize(values, gain, shift):
@@ -48,7 +64,7 @@
     gathered = (
         lax.all_gather(w_qkv.astype(low_type), "dp", axis=0, tiled=True),
         lax.all_gather(w_proj.astype(low_type), "dp", axis=1, tiled=True),
-        lax.all_gather(w_up.astype(low_type), "dp", axis=0, tiled=True),
+        ring_gather(w_up.astype(low_type), "dp", 0),
         lax.all_gather(w_down.astype(low_type), "dp", axis=1, tiled=True),
         lax.all_gather(attn_gain.astype(low_type), "dp", axis=0, tiled=True),
         lax.all_gather(attn_shift.astype(low_type), "dp", axis=0, tiled=True),

time: 1080 us -> 1040 us (0.963)
  waiting for transfers between devices: 525 us -> 442 us
  starting transfers between devices: 0.8 us -> 32.2 us
  local copies, waits for them, and re-layouts: 53.1 us -> 66.3 us
    psum x1, waiting for transfers between devices: 83.8 us -> 24.4 us  [per_device(): lax.psum(proj_part.astype(jnp.bfloat16), 'mp').astype(jnp.float32)]
    all_gather x1 -> x0, waiting for transfers between devices: 38.6 us -> none  [per_device(): lax.all_gather(w_up.astype(low_type), 'dp', axis=0, tiled=True)]
    ppermute x0 -> x15, starting transfers between devices: none -> 31.3 us  [the longest x7 30.7 us: ring_gather(): lax.ppermute(going_down, axis, [(d, (d - 1) % ways) for d in range(ways)])]
    ppermute x0 -> x15, waiting for transfers between devices: none -> 13.7 us  [the longest x8 13.7 us: ring_gather(): lax.ppermute(going_up, axis, [(d, (d + 1) % ways) for d in range(ways)])]
    dynamic_update_slice x0 -> x15, local copies, waits for them, and re-layouts: none -> 11.9 us  [the longest x8 6.28 us: ring_gather(): lax.dynamic_update_slice_in_dim(full, going_up, (here - far) % ways * hop...]
    unnamed x103 -> x105, local copies, waits for them, and re-layouts: 23.1 us -> 23.1 us
  transfers between devices with their start and end apart: 10 -> 24, of which waited for: 7 -> 12; matrix products, arithmetic and copies ran while one was open for 16% -> 17% of each run, Pallas kernels for 0% -> 0%
where the time goes in v1:
time: 1040 us; the launch traced here: 1030 us
  waiting for transfers between devices  442 us (42%)
  matrix products  192 us (18%)
  blocking collectives  145 us (14%)
  other arithmetic  136 us (13%)
  local copies, waits for them, and re-layouts  66.3 us (6%)
  starting transfers between devices  32.2 us (3%)
  between operations  16.2 us (2%)
    unnamed x2, blocking collectives  125 us
    psum x1, waiting for transfers between devices, per_device(): mlp_sum = lax.psum(down_part.astype(jnp.bfloat16), 'mp').astype(jnp.float32)  115 us
    psum x1, waiting for transfers between devices, per_device(): lax.psum(jnp.einsum('psf,df->psd', d_pre, up_back, preferred_element_type...  82.4 us
    reduce_scatter x1, waiting for transfers between devices, per_device(): lax.psum_scatter(grad_w_down, 'dp', scatter_dimension=1, tiled=True)  79.2 us
    reduce_scatter x1, waiting for transfers between devices, per_device(): lax.psum_scatter(grad_w_qkv, 'dp', scatter_dimension=0, tiled=True)  71.9 us
    reduce_scatter x1, waiting for transfers between devices, per_device(): lax.psum_scatter(grad_w_up, 'dp', scatter_dimension=0, tiled=True)  54.5 us
    convert_element_type x1, other arithmetic, per_device(): active = jax.nn.gelu(pre_act, approximate=False).astype(low_type)  33.2 us
    ppermute x7, starting transfers between devices, ring_gather(): lax.ppermute(going_down, axis, [(d, (d - 1) % ways) for d in range(ways)])  30.7 us
  transfers between devices with their start and end apart: 24, of which 12 were waited for; matrix products, arithmetic and copies ran while one was open for 17% of the time, Pallas kernels for 0%

profile of v1, /device:TPU:0, one launch (start us, length us, event | category | flops | bytes accessed | tf_op | source)
XLA Modules:
  0.0 1029.6 jit_solution(835731046980263757)
XLA Ops:
  20.8 63.2 %all-reduce.13 = (bf16[768]{0:T(1024)(128)(2,1)}, bf16[768]{0:T(1024)(128)(2,1)}, bf16[768]{0:T(1024)(128)(2,1)}, bf16[768]{0:T(1024)(128)(2,1)}, bf16[768]{0:T(1024)(128)(2,1)}, /*index=5*/bf16[768]{0:T(1024)(128)(2,1)}) all-reduce(bf16[768]{0:T(1024)(128)(2,1)} %dynamic-update-slice.4, ...), channel_id=1, replica_groups=mesh['dp'=16,'mp'=2] {'dp'}, use_global_device_ids=true, to_apply=%add.4 | all-reduce | flops 4608 | bytes 18432
  97.2 20.3 %all_gather.30 = bf16[384,768]{0,1:T(8,128)(2,1)} all-gather(bf16[384,48]{0,1:T(8,128)(2,1)S(1)} %convert_element_type.183), channel_id=1, replica_groups=mesh['dp'=16,'mp'=2] {'dp'}, dimensions={1}, use_global_device_ids=true | all-gather | bytes 626688 | tf_op jit(solution)/shard_map/all_gather | solution.py:66
  117.5 7.1 fusion.96
  129.3 5.7 copy.58
  135.0 5.5 copy.59
  144.5 7.3 add_convert_fusion.3
  151.8 32.6 %while.22 = (s32[]{:T(128)}, bf16[4,2,280,6,64]{2,4,3,1,0:T(8,128)(2,1)}, f32[4,2,6,280]{3,2,1,0:T(8,128)S(1)}, bf16[4,2,280,6,64]{2,4,3,1,0:T(8,128)(2,1)}, f32...) while((s32[]{:T(128)}, ...), condition=%wide.region_5.6_spmd, body=%wide.region_2.5_spmd.sunk | while | flops 252346640 | bytes 13796445 | solution.py:122
  184.4 6.0 convolution_convert_fusion.2
  250.5 5.9 collective-permute-done.14
  257.1 24.4 %all-reduce.19.cloned.1.call-done = bf16[8,280,768]{2,1,0:T(8,128)(2,1)} async-done(((bf16[8,280,768]{2,1,0:T(8,128)(2,1)}), bf16[8,280,768]{2,1,0:T(8,128)(2,1)}) %all-reduce.19.cloned.1.call-update) | async-done | bytes 3440656 | tf_op jit(solution)/shard_map/psum | solution.py:127
  287.4 12.6 %fusion.86 = (u8[280,1536]{1,0:T(8,128)(4,1)S(1)}, u8[280,1536]{1,0:T(8,128)(4,1)S(1)}, f32[8,280,1536]{2,1,0:T(8,128)S(1)}) fusion(f32[1536]{0:T(1024)S(1)} %copy-done.27, bf16[768,1536]{1,0:T(8,128)(2,1)} %constant_dynamic-update-slice_fusion, f32[768]{0:T(1024)S(1)} %copy-done.37, f32[768]{0:T(1024)S(1)} %copy-done.24, f32[8,280]{1,0:T(8,128)S(1)} %fusion.110, ...), kind=kOutput, calls=%fused_computation.134 | convolution fusion | flops 5347614720 | bytes 23896576 | tf_op jit(solution)/shard_map/psd,df->psf/dot_general | solution.py:131
  300.1 5.0 copy-done.6
  305.1 33.2 %multiply_convert_fusion.1 = (bf16[8,280,1536]{2,1,0:T(8,128)(2,1)}, f32[8,280,1536]{2,1,0:T(8,128)}) fusion(f32[8,280,1536]{2,1,0:T(8,128)S(1)} %get-tuple-element.189, f32[1536]{0:T(1024)S(1)} %copy-done.27, u8[280,1536]{1,0:T(8,128)(4,1)S(1)} %get-tuple-element.113, u8[280,1536]{1,0:T(8,128)(4,1)S(1)} %get-tuple-element.112), kind=kLoop, calls=%fused_computation.75 | loop fusion | flops 244285440 | bytes 35272704 | tf_op jit(solution)/shard_map/convert_element_type | solution.py:133
  338.3 18.4 %convert_reduce_fusion.1 = (f32[1536]{0:T(1024)}, bf16[8,280,1536]{2,1,0:T(8,128)(2,1)}) fusion(f32[8,280,1536]{2,1,0:T(8,128)} %get-tuple-element.173, bf16[1536,768]{0,1:T(8,128)(2,1)} %all-gather.5.cloned.1.call-done, bf16[8,280,768]{2,1,0:T(8,128)(2,1)} %param.21, f32[8,280]{1,0:T(8,128)} %fusion.108, f32[8,280,1536]{2,1,0:T(8,128)} %copy-done.6, ...), kind=kOutput, calls=%fused_computation.73 | convolution fusion | flops 5348473344 | bytes 40227584 | tf_op jit(solution)/shard_map/psd,fd->psf/dot_general | solution.py:145
  356.8 9.7 convolution_convert_fusion
  366.5 9.9 convolution_convert_fusion.1
  376.5 82.4 %all-reduce.21.cloned.1.call-done = bf16[8,280,768]{2,1,0:T(8,128)(2,1)} async-done(((bf16[8,280,768]{2,1,0:T(8,128)(2,1)}), bf16[8,280,768]{2,1,0:T(8,128)(2,1)}) %all-reduce.21.cloned.1.call-update) | async-done | bytes 3440656 | tf_op jit(solution)/shard_map/psum | solution.py:152
  458.9 6.3 convert_reduce_fusion.3
  465.3 5.6 fusion.77
  470.8 4.9 fusion.111
  485.6 63.8 %while.23 = (s32[]{:T(128)}, bf16[4,2,280,3,6,64]{2,5,4,1,3,0:T(8,128)(2,1)}, bf16[4,2,280,6,64]{2,4,3,1,0:T(8,128)(2,1)}, f32[4,2,280]{2,1,0:T(2,128)}, bf16[4,...) while((s32[]{:T(128)}, ...), condition=%wide.region_15.16_spmd, body=%wide.region_13.15_spmd.sunk | while | flops 621167104 | bytes 36805476 | solution.py:192
  556.6 7.7 bitcast_convert_fusion
  564.8 7.4 fusion.101
  572.3 12.6 %convolution_bitcast_fusion.1 = f32[768,1536]{1,0:T(8,128)} fusion(bf16[8,280,1536]{2,1,0:T(8,128)(2,1)} %get-tuple-element.191, f32[768]{0:T(1024)S(1)} %copy-done.38, f32[768]{0:T(1024)S(1)} %copy-done.26, f32[8,280]{1,0:T(8,128)S(1)} %copy-done.21, f32[8,280]{1,0:T(8,128)S(1)} %broadcast_multiply_fusion, f32[768]{0:T(1024)S(1)} %convert_element_type.187, ...), kind=kOutput, calls=%fused_computation.130 | convolution fusion | flops 5300305920 | bytes 18508288 | tf_op jit(solution)/shard_map/psd,psf->df/dot_general | solution.py:151
  584.9 11.0 %convolution_bitcast_fusion = f32[1536,768]{0,1:T(8,128)} fusion(bf16[8,280,1536]{2,1,0:T(8,128)(2,1)} %get-tuple-element.172, bf16[8,280,768]{2,1,0:T(8,128)(2,1)} %param.21, f32[8,280]{1,0:T(8,128)S(1)} %copy-done.18), kind=kOutput, calls=%fused_computation.129 | convolution fusion | flops 5289984000 | bytes 15049472 | tf_op jit(solution)/shard_map/psf,psd->fd/dot_general | solution.py:142
  596.2 13.8 %convolution_bitcast_fusion.2 = f32[768,3,384]{2,0,1:T(8,128)} fusion(bf16[8,280,3,384]{1,3,2,0:T(8,128)(2,1)} %bitcast.170, bf16[8,280,768]{2,1,0:T(8,128)(2,1)S(1)} %copy-done, f32[768]{0:T(1024)S(1)} %copy-done.36, f32[768]{0:T(1024)S(1)} %copy-done.23, f32[8,280]{1,0:T(8,128)S(1)} %copy-done.16, f32[8,280]{1,0:T(8,128)S(1)} %copy-done.11), kind=kOutput, calls=%fused_computation.144 | convolution fusion | flops 3973939200 | bytes 12164608 | tf_op jit(solution)/shard_map/psd,pstc->dtc/dot_general | solution.py:206
  615.1 115.3 %all-reduce.23.cloned.1.call-done = (bf16[8,280,768]{2,1,0:T(8,128)(2,1)}, bf16[8,280,768]{2,1,0:T(8,128)(2,1)}) async-done(((bf16[8,280,768]{2,1,0:T(8,128)(2,1)}, bf16[8,280,768]{2,1,0:T(8,128)(2,1)}), (bf16[8,280,768]{2,1,0:T(8,128)(2,1)}, bf16[8,280,768]{2,1,0:T(8,128)(2,1)})) %all-reduce.23.cloned.1.call-update) | async-done | bytes 6881296 | tf_op jit(solution)/shard_map/psum | solution.py:135
  739.0 61.8 %all-reduce.12 = (f32[768]{0:T(1024)S(1)}, f32[768]{0:T(1024)S(1)}, f32[2,384]{1,0:T(2,128)}, f32[768]{0:T(1024)}, f32[768]{0:T(1024)}, /*index=5*/f32[768]{0:T(1024)}, f32[1536]{0:T(1024)}, f32[768]{0:T(1024)S(1)}) all-reduce(f32[768]{0:T(1024)S(1)} %get-tuple-element.116, ...), channel_id=2, replica_groups=mesh['dp'=16,'mp'=2] {'dp'}, use_global_device_ids=true, to_apply=%region_20.21.clone | all-reduce | flops 6912 | bytes 55296
  806.4 11.0 %add_convert_fusion.1 = (bf16[8,280,768]{2,1,0:T(8,128)(2,1)}, bf16[8,280,768]{2,1,0:T(8,128)(2,1)}) fusion(f32[8,280,768]{2,1,0:T(8,128)} %copy-done.3, bf16[8,280,768]{2,1,0:T(8,128)(2,1)S(1)} %copy-done, bf16[8,280,768]{2,1,0:T(8,128)(2,1)} %get-tuple-element.169, f32[8,280]{1,0:T(8,128)S(1)} %negate_multiply_fusion.1, ...), kind=kLoop, calls=%fused_computation.116 | loop fusion | flops 32686080 | bytes 27579136 | tf_op jit(solution)/shard_map/convert_element_type | solution.py:214
  817.4 54.5 %reduce-scatter.9.cloned.1.call-done = f32[48,1536]{1,0:T(8,128)} async-done(((f32[768,1536]{1,0:T(8,128)}), f32[48,1536]{1,0:T(8,128)}) %reduce-scatter.9.cloned.1.call-update) | async-done | bytes 294928 | tf_op jit(solution)/shard_map/reduce_scatter | solution.py:219
  871.8 79.2 %reduce-scatter.11.cloned.1.call-done = f32[1536,48]{0,1:T(8,128)} async-done(((f32[1536,768]{0,1:T(8,128)}), f32[1536,48]{0,1:T(8,128)}) %reduce-scatter.11.cloned.1.call-update) | async-done | bytes 294928 | tf_op jit(solution)/shard_map/reduce_scatter | solution.py:220
  951.0 71.9 %reduce-scatter.5.cloned.1.call-done = f32[48,3,384]{2,0,1:T(8,128)} async-done(((f32[768,3,384]{2,0,1:T(8,128)}), f32[48,3,384]{2,0,1:T(8,128)}) %reduce-scatter.5.cloned.1.call-update) | async-done | bytes 221200 | tf_op jit(solution)/shard_map/reduce_scatter | solution.py:217
  (279 shorter events, 233.6 us)
Async XLA Ops:
  7.2 110.4 %copy-start = (bf16[8,280,768]{2,1,0:T(8,128)(2,1)S(1)}, bf16[8,280,768]{2,1,0:T(8,128)(2,1)}, u32[]{:S(2)}) copy-start(bf16[8,280,768]{2,1,0:T(8,128)(2,1)} %param.20) | copy-start | bytes 10321924
  7.2 110.3 %all-gather.3.cloned.1.call-start = ((), (), s32[]{:S(2)}) async-start(), calls=%async_computation.4 | async-start | bytes 1880064 | tf_op jit(solution)/shard_map/all_gather | solution.py:65
  9.0 272.5 %all-reduce.19.cloned.1.call-start = ((), (), s32[]{:S(2)}) async-start(), calls=%async_computation.5 | async-start | bytes 6881280 | tf_op jit(solution)/shard_map/psum | solution.py:127
  84.7 39.9 %copy-start.22 = (f32[768]{0:T(1024)}, f32[768]{0:T(1024)S(1)}, u32[]{:S(2)}) copy-start(f32[768]{0:T(1024)S(1)} %convert_element_type.172) | copy-start | bytes 9220
  92.9 31.7 %copy-start.10 = (f32[8,280]{1,0:T(8,128)}, f32[8,280]{1,0:T(8,128)S(1)}, u32[]{:S(2)}) copy-start(f32[8,280]{1,0:T(8,128)S(1)} %broadcast_multiply_fusion.1) | copy-start | bytes 26884
  184.4 17.7 %copy-start.40 = (bf16[768]{0:T(1024)(128)(2,1)S(1)}, bf16[768]{0:T(1024)(128)(2,1)}, u32[]{:S(2)}) copy-start(bf16[768]{0:T(1024)(128)(2,1)} %get-tuple-element.162) | copy-start | bytes 4612
  184.4 18.3 %copy-start.34 = (f32[1536]{0:T(1024)S(1)}, f32[1536]{0:T(1024)}, u32[]{:S(2)}) copy-start(f32[1536]{0:T(1024)} %param.31) | copy-start | bytes 18436
  190.4 147.9 %all-gather.5.cloned.1.call-start = ((), (), s32[]{:S(2)}) async-start(), calls=%async_computation.6 | async-start | bytes 2506752 | tf_op jit(solution)/shard_map/all_gather | solution.py:68
  193.7 10.9 %collective-permute-start = (bf16[48,1536]{1,0:T(8,128)(2,1)}, bf16[48,1536]{1,0:T(8,128)(2,1)}, u32[]{:S(2)}, u32[]{:S(2)}) collective-permute-start(bf16[48,1536]{1,0:T(8,128)(2,1)} %get-tuple-element.175), channel_id=1, source_target_pairs={{0,2},{2,4},{4,6},{6,8},{8,10},{10,12},{12,14},{14,16},{16,18},{18... | collective-permute-start | bytes 442376 | tf_op jit(solution)/shard_map/ppermute | solution.py:18
  194.1 10.5 %collective-permute-start.1 = (bf16[48,1536]{1,0:T(8,128)(2,1)}, bf16[48,1536]{1,0:T(8,128)(2,1)}, u32[]{:S(2)}, u32[]{:S(2)}) collective-permute-start(bf16[48,1536]{1,0:T(8,128)(2,1)} %get-tuple-element.175), channel_id=1, source_target_pairs={{0,30},{2,0},{4,2},{6,4},{8,6},{10,8},{12,10},{14,12},{16,14},{18,... | collective-permute-start | bytes 442376 | tf_op jit(solution)/shard_map/ppermute | solution.py:21
  199.8 259.0 %all-reduce.21.cloned.1.call-start = ((), (), s32[]{:S(2)}) async-start(), calls=%async_computation.7 | async-start | bytes 6881280 | tf_op jit(solution)/shard_map/psum | solution.py:152
  204.6 7.6 collective-permute-start.2
  204.6 7.6 collective-permute-start.3
  212.2 7.4 collective-permute-start.4
  212.2 7.4 collective-permute-start.5
  219.6 7.4 collective-permute-start.6
  219.6 7.4 collective-permute-start.7
  227.0 7.4 collective-permute-start.8
  227.0 7.4 collective-permute-start.9
  234.3 7.4 collective-permute-start.10
  234.3 7.4 collective-permute-start.11
  241.7 7.3 collective-permute-start.12
  241.7 8.1 collective-permute-start.13
  249.0 7.5 collective-permute-start.14
  366.5 364.0 %all-reduce.23.cloned.1.call-start = ((), (), s32[]{:S(2)}) async-start(), calls=%async_computation.12 | async-start | bytes 13762560 | tf_op jit(solution)/shard_map/psum | solution.py:135
  564.3 253.0 %reduce-scatter.7.cloned.1.call-start = ((), (), s32[]{:S(2)}) async-start(), calls=%async_computation.9 | async-start | bytes 1253376 | tf_op jit(solution)/shard_map/reduce_scatter | solution.py:218
  572.2 12.8 %copy-start.18 = (f32[8,280]{1,0:T(8,128)S(1)}, f32[8,280]{1,0:T(8,128)}, u32[]{:S(2)}) copy-start(f32[8,280]{1,0:T(8,128)} %fusion.108) | copy-start | bytes 26884
  572.2 299.6 %reduce-scatter.9.cloned.1.call-start = ((), (), s32[]{:S(2)}) async-start(), calls=%async_computation.10 | async-start | bytes 5013504 | tf_op jit(solution)/shard_map/reduce_scatter | solution.py:219
  584.9 366.1 %reduce-scatter.11.cloned.1.call-start = ((), (), s32[]{:S(2)}) async-start(), calls=%async_computation.11 | async-start | bytes 5013504 | tf_op jit(solution)/shard_map/reduce_scatter | solution.py:220
  595.9 14.1 %copy-start.39 = (bf16[768]{0:T(1024)(128)(2,1)S(1)}, bf16[768]{0:T(1024)(128)(2,1)}, u32[]{:S(2)}) copy-start(bf16[768]{0:T(1024)(128)(2,1)} %get-tuple-element.167) | copy-start | bytes 4612
  595.9 427.0 %reduce-scatter.5.cloned.1.call-start = ((), (), s32[]{:S(2)}) async-start(), calls=%async_computation.8 | async-start | bytes 3760128 | tf_op jit(solution)/shard_map/reduce_scatter | solution.py:217
  610.7 124.0 %copy-start.13 = (f32[8,280]{1,0:T(8,128)S(1)}, f32[8,280]{1,0:T(8,128)}, u32[]{:S(2)}) copy-start(f32[8,280]{1,0:T(8,128)} %copy-done.12) | copy-start | bytes 26884
  (35 other events, 231.9 us)
Sparse Core Ops, SparseCore 0:
  10.9 43.1 all-gather.2
  190.6 90.9 all-reduce.18
  284.4 42.3 all-gather.4
  366.6 92.2 all-reduce.20
  564.4 165.9 all-reduce.22
  734.5 58.2 reduce-scatter.6
  797.2 74.6 reduce-scatter.8
  876.3 74.7 reduce-scatter.10
  955.5 67.3 reduce-scatter.4
